TPU v7x, 256 devices: a whole 4x4x8 slice. The times are simulated.
256 devices in a mesh: section: 8 (over y, core), rows: 32 (over x, z).
Axes of the slice: x: 4, y: 4, z: 8, core: 2. Of those that a mesh axis runs over, the one named last changes fastest.
Arguments:
- grad_in: bfloat16 [8, 8192, 256], P('section', 'rows'), may hold values from -6 to 6
- grad_last: bfloat16 [8192, 256], P('rows'), may hold values from -6 to 6
- support: bfloat16 [8, 2, 2, 8192, 256], P('section', None, None, 'rows'), may hold values from -6 to 6
- preact: bfloat16 [8, 2, 2, 8192, 256], P('section', None, None, 'rows'), may hold values from -6 to 6
- weights: bfloat16 [8, 2, 256, 256], P('section'), may hold values from -0.375 to 0.375
- tile_vals: bfloat16 [8, 2, 3072, 128, 128], P('section', None, 'rows'), may hold values from -0.078125 to 0.078125
- tile_row: int32 [8, 2, 3072], P('section', None, 'rows'), may hold values from 0 to 1
- tile_col: int32 [8, 2, 3072], P('section', None, 'rows'), may hold values from 0 to 63, as said below
- tile_count: int32 [8, 2, 32], P('section', None, 'rows'), may hold values from 48 to 96, as said below
Outputs:
- handoff: bfloat16 [2, 8, 8192, 256], P(None, 'section', 'rows')
- init_grad: float32 [8, 2, 8192, 256], P('section', None, 'rows')
- weight_grad: float32 [8, 2, 256, 256], P('section')
Inputs may be any that keep to these rules, and one draw needn't show every extreme that they name: tile_count[s, t, d] is the number of live entries in device d's list; in every section and micro-batch some device has all 96 live. `tile_col`: for every section, micro-batch and pair of devices d and o with o != d, all entries of device d's list (live or padding) whose column tile lies in device o's rows name one and the same of o's 2 row tiles.
All inputs are finite; a program needn't handle non-finite values.
Results may differ from a plain program's by a relative error of at most 0.0066.
Values may be sent and summed in bfloat16 or wider, within the bound.
A program may use at most 128 MiB of HBM per device.

v0:
```python
import jax
import jax.numpy as jnp
from jax import lax
from jax.sharding import PartitionSpec as P

ALPHA = 0.1
BETA_SCALE = 0.5


def passed_along(block, axis, distance):
    devices = range(lax.axis_size(axis))
    route = [(i - distance, i) for i in devices if i - distance in devices]
    return lax.ppermute(block, axis, route)


def tile_product(gathered, values, row_local, index, count, row_tiles):
    tile = values.shape[-1]
    width = gathered.shape[-1]
    blocks = gathered.reshape(-1, tile, width)[index]
    products = jnp.einsum("kab,kbf->kaf", values, blocks, preferred_element_type=jnp.float32)
    live = jnp.arange(index.shape[0]) < count
    select = ((row_local[None, :] == jnp.arange(row_tiles)[:, None]) & live[None, :]).astype(
        jnp.float32
    )
    summed = jnp.einsum("ik,kaf->iaf", select, products, precision=lax.Precision.HIGHEST)
    return summed.reshape(row_tiles * tile, width)


def shards(grad_in, grad_last, support, preact, weights, tile_vals, tile_row, tile_col, tile_count):
    section = lax.axis_index("section")
    sections = lax.axis_size("section")
    ticks = support.shape[1]
    layers = support.shape[2]
    rows_dev, width = grad_last.shape
    tile = tile_vals.shape[-1]
    row_tiles = rows_dev // tile
    weight_acc = [jnp.zeros((width, width), jnp.float32) for layer in range(layers)]
    handed = []
    initial = []
    for tick in range(ticks):
        if tick == 0:
            grad = grad_in[0]
        else:
            passed = passed_along(handed[-1], "section", -1)
            grad = jnp.where(section == sections - 1, grad_last, passed)
        columns = tile_col[0, tick]
        count = tile_count[0, tick, 0]
        toward = jnp.zeros((rows_dev, width), jnp.float32)
        for layer in reversed(range(layers)):
            beta = jnp.log(BETA_SCALE / (layers * section + layer + 1).astype(jnp.float32) + 1.0)
            weight = weights[0, layer]
            masked = jnp.where(preact[0, tick, layer] > 0, grad, jnp.zeros_like(grad))
            term = beta * jnp.dot(
                support[0, tick, layer].T, masked, preferred_element_type=jnp.float32
            )
            weight_acc[layer] = weight_acc[layer] + lax.psum(term, "rows")
            image = (
                (1.0 - beta) * masked.astype(jnp.float32)
                + beta * jnp.dot(masked, weight.T, preferred_element_type=jnp.float32)
            ).astype(jnp.bfloat16)
            toward = toward + ALPHA * image.astype(jnp.float32)
            gathered = lax.all_gather(image, "rows", axis=0, tiled=True)
            spread = tile_product(
                gathered, tile_vals[0, tick], tile_row[0, tick], columns, count, row_tiles
            )
            grad = ((1.0 - ALPHA) * spread).astype(jnp.bfloat16)
        handed.append(grad)
        initial.append(toward)
    return (jnp.stack(handed)[:, None], jnp.stack(initial)[None], jnp.stack(weight_acc)[None])


def solution(mesh):
    return jax.shard_map(
        shards,
        mesh=mesh,
        in_specs=(
            P("section", "rows", None),
            P("rows", None),
            P("section", None, None, "rows", None),
            P("section", None, None, "rows", None),
            P("section", None, None, None),
            P("section", None, "rows", None, None),
            P("section", None, "rows"),
            P("section", None, "rows"),
            P("section", None, "rows"),
        ),
        out_specs=(
            P(None, "section", "rows", None),
            P("section", None, "rows", None),
            P("section", None, None, None),
        ),
        check_vma=False,
    )
```

profile of v0, /device:TPU:8, one launch (start us, length us, event | category | flops | bytes accessed | tf_op | source)
XLA Modules:
  0.0 648.4 jit_solution(17739819495514293798)
XLA Ops:
  7.3 2.1 fusion.15
  13.0 82.8 %all-gather.5.cloned.1.call-done = bf16[8192,256]{1,0:T(8,128)(2,1)} async-done(((bf16[256,256]{1,0:T(8,128)(2,1)}), bf16[8192,256]{1,0:T(8,128)(2,1)}) %all-gather.5.cloned.1.call-update) | async-done | bytes 4194320 | tf_op jit(solution)/shard_map/all_gather | solution.py:62
  95.8 8.1 %gather_fusion = bf16[96,128,256]{2,1,0:T(8,128)(2,1)} fusion(bf16[64,128,256]{2,1,0:T(8,128)(2,1)} %bitcast.141, s32[1024]{0:T(1024)S(1)} %pad_clamp_fusion.1), kind=kCustom, calls=%fused_computation | custom fusion | bytes 12583296 | tf_op jit(solution)/shard_map/gather | solution.py:19
  103.9 10.1 %convolution_bitcast_fusion.3 = f32[96,128,256]{1,2,0:T(8,128)} fusion(bf16[96,128,256]{2,1,0:T(8,128)(2,1)} %gather_fusion, bf16[1,2,96,128,128]{4,3,2,1,0:T(8,128)(2,1)} %param.14), kind=kOutput, calls=%fused_computation.7 | convolution fusion | flops 805306368 | bytes 22020096 | tf_op jit(solution)/shard_map/kab,kbf->kaf/dot_general | solution.py:20
  114.0 12.8 %copy.38 = f32[96,128,256]{2,0,1:T(8,128)} copy(f32[96,128,256]{1,2,0:T(8,128)} %convolution_bitcast_fusion.3) | data formatting | bytes 25165824 | tf_op jit(solution)/shard_map/kab,kbf->kaf/dot_general | solution.py:20
  126.7 7.1 %fusion.65 = f32[2,128,256]{2,0,1:T(2,128)S(1)} fusion(f32[96,128,256]{2,0,1:T(8,128)} %copy.38, pred[96]{0:T(512)(128)(4,1)S(1)} %iota_compare_fusion.1, s32[96]{0:T(128)S(1)} %get-tuple-element.18), kind=kOutput, calls=%fused_computation.97 | convolution fusion | flops 75497856 | bytes 12845536 | tf_op jit(solution)/shard_map/ik,kaf->iaf/dot_general | solution.py:25
  135.0 78.9 %all-gather.7.cloned.1.call-done = bf16[8192,256]{1,0:T(8,128)(2,1)} async-done(((bf16[256,256]{1,0:T(8,128)(2,1)}), bf16[8192,256]{1,0:T(8,128)(2,1)}) %all-gather.7.cloned.1.call-update) | async-done | bytes 4194320 | tf_op jit(solution)/shard_map/all_gather | solution.py:62
  213.9 8.1 %gather_fusion.1 = bf16[96,128,256]{2,1,0:T(8,128)(2,1)} fusion(bf16[64,128,256]{2,1,0:T(8,128)(2,1)} %bitcast.144, s32[1024]{0:T(1024)S(1)} %pad_clamp_fusion.1), kind=kCustom, calls=%fused_computation.1 | custom fusion | bytes 12583296 | tf_op jit(solution)/shard_map/gather | solution.py:19
  222.0 10.1 %convolution_bitcast_fusion.2 = f32[96,128,256]{1,2,0:T(8,128)} fusion(bf16[96,128,256]{2,1,0:T(8,128)(2,1)} %gather_fusion.1, bf16[1,2,96,128,128]{4,3,2,1,0:T(8,128)(2,1)} %param.14), kind=kOutput, calls=%fused_computation.6 | convolution fusion | flops 805306368 | bytes 22020096 | tf_op jit(solution)/shard_map/kab,kbf->kaf/dot_general | solution.py:20
  232.1 12.8 %copy.41 = f32[96,128,256]{2,0,1:T(8,128)} copy(f32[96,128,256]{1,2,0:T(8,128)} %convolution_bitcast_fusion.2) | data formatting | bytes 25165824 | tf_op jit(solution)/shard_map/kab,kbf->kaf/dot_general | solution.py:20
  244.9 7.1 %fusion.63 = f32[2,128,256]{2,0,1:T(2,128)S(1)} fusion(f32[96,128,256]{2,0,1:T(8,128)} %copy.41, pred[96]{0:T(512)(128)(4,1)S(1)} %iota_compare_fusion.1, s32[96]{0:T(128)S(1)} %get-tuple-element.18), kind=kOutput, calls=%fused_computation.95 | convolution fusion | flops 75497856 | bytes 12845536 | tf_op jit(solution)/shard_map/ik,kaf->iaf/dot_general | solution.py:25
  252.0 1.9 collective-permute-start
  253.9 2.5 collective-permute-done
  259.7 78.0 %all-gather.9.cloned.1.call-done = bf16[8192,256]{1,0:T(8,128)(2,1)} async-done(((bf16[256,256]{1,0:T(8,128)(2,1)}), bf16[8192,256]{1,0:T(8,128)(2,1)}) %all-gather.9.cloned.1.call-update) | async-done | bytes 4194320 | tf_op jit(solution)/shard_map/all_gather | solution.py:62
  337.7 8.1 %gather_fusion.2 = bf16[96,128,256]{2,1,0:T(8,128)(2,1)} fusion(bf16[64,128,256]{2,1,0:T(8,128)(2,1)} %bitcast.143, s32[1024]{0:T(1024)S(1)} %pad_clamp_fusion), kind=kCustom, calls=%fused_computation.2 | custom fusion | bytes 12583296 | tf_op jit(solution)/shard_map/gather | solution.py:19
  345.8 10.1 %convolution_bitcast_fusion.1 = f32[96,128,256]{1,2,0:T(8,128)} fusion(bf16[96,128,256]{2,1,0:T(8,128)(2,1)} %gather_fusion.2, bf16[1,2,96,128,128]{4,3,2,1,0:T(8,128)(2,1)} %param.14), kind=kOutput, calls=%fused_computation.5 | convolution fusion | flops 805306368 | bytes 22020096 | tf_op jit(solution)/shard_map/kab,kbf->kaf/dot_general | solution.py:20
  355.9 12.8 %copy.44 = f32[96,128,256]{2,0,1:T(8,128)} copy(f32[96,128,256]{1,2,0:T(8,128)} %convolution_bitcast_fusion.1) | data formatting | bytes 25165824 | tf_op jit(solution)/shard_map/kab,kbf->kaf/dot_general | solution.py:20
  368.6 7.0 %fusion.61 = f32[2,128,256]{2,0,1:T(2,128)S(1)} fusion(f32[96,128,256]{2,0,1:T(8,128)} %copy.44, pred[96]{0:T(512)(128)(4,1)S(1)} %iota_compare_fusion, s32[96]{0:T(128)S(1)} %get-tuple-element.17), kind=kOutput, calls=%fused_computation.93 | convolution fusion | flops 75497856 | bytes 12845536 | tf_op jit(solution)/shard_map/ik,kaf->iaf/dot_general | solution.py:25
  379.8 141.9 %all-reduce.3.cloned.1.call-done = (f32[256,256]{0,1:T(8,128)}, f32[256,256]{0,1:T(8,128)}) async-done(((f32[256,256]{0,1:T(8,128)}, f32[256,256]{0,1:T(8,128)}), (f32[256,256]{0,1:T(8,128)}, f32[256,256]{0,1:T(8,128)})) %all-reduce.3.cloned.1.call-update) | async-done | bytes 524304 | tf_op jit(solution)/shard_map/psum | solution.py:56
  523.7 79.4 %all-gather.11.cloned.1.call-done = bf16[8192,256]{1,0:T(8,128)(2,1)} async-done(((bf16[256,256]{1,0:T(8,128)(2,1)}), bf16[8192,256]{1,0:T(8,128)(2,1)}) %all-gather.11.cloned.1.call-update) | async-done | bytes 4194320 | tf_op jit(solution)/shard_map/all_gather | solution.py:62
  603.1 8.1 %gather_fusion.3 = bf16[96,128,256]{2,1,0:T(8,128)(2,1)} fusion(bf16[64,128,256]{2,1,0:T(8,128)(2,1)} %bitcast.142, s32[1024]{0:T(1024)S(1)} %pad_clamp_fusion), kind=kCustom, calls=%fused_computation.3 | custom fusion | bytes 12583296 | tf_op jit(solution)/shard_map/gather | solution.py:19
  611.2 10.1 %convolution_bitcast_fusion = f32[96,128,256]{1,2,0:T(8,128)} fusion(bf16[96,128,256]{2,1,0:T(8,128)(2,1)} %gather_fusion.3, bf16[1,2,96,128,128]{4,3,2,1,0:T(8,128)(2,1)} %param.14), kind=kOutput, calls=%fused_computation.4 | convolution fusion | flops 805306368 | bytes 22020096 | tf_op jit(solution)/shard_map/kab,kbf->kaf/dot_general | solution.py:20
  621.3 12.8 %copy.47 = f32[96,128,256]{2,0,1:T(8,128)} copy(f32[96,128,256]{1,2,0:T(8,128)} %convolution_bitcast_fusion) | data formatting | bytes 25165824 | tf_op jit(solution)/shard_map/kab,kbf->kaf/dot_general | solution.py:20
  634.1 7.0 %fusion.59 = f32[2,128,256]{2,0,1:T(2,128)S(1)} fusion(f32[96,128,256]{2,0,1:T(8,128)} %copy.47, pred[96]{0:T(512)(128)(4,1)S(1)} %iota_compare_fusion, s32[96]{0:T(128)S(1)} %get-tuple-element.17), kind=kOutput, calls=%fused_computation.91 | convolution fusion | flops 75497856 | bytes 12845536 | tf_op jit(solution)/shard_map/ik,kaf->iaf/dot_general | solution.py:25
  (51 shorter events, 14.8 us)
Async XLA Ops:
  7.2 88.6 %all-gather.5.cloned.1.call-start = ((), (), s32[]{:S(2)}) async-start(), calls=%async_computation | async-start | bytes 4325376 | tf_op jit(solution)/shard_map/all_gather | solution.py:62
  9.4 204.6 %all-gather.7.cloned.1.call-start = ((), (), s32[]{:S(2)}) async-start(), calls=%async_computation.1 | async-start | bytes 4325376 | tf_op jit(solution)/shard_map/all_gather | solution.py:62
  126.7 7.1 %copy-start = (bf16[1,2,2,256,256]{4,3,2,1,0:T(8,128)(2,1)S(1)}, bf16[1,2,2,256,256]{4,3,2,1,0:T(8,128)(2,1)}, u32[]{:S(2)}) copy-start(bf16[1,2,2,256,256]{4,3,2,1,0:T(8,128)(2,1)} %param.12) | copy-start | bytes 1572868
  126.7 7.1 %copy-start.7 = (bf16[1,2,256,256]{3,2,1,0:T(8,128)(2,1)S(1)}, bf16[1,2,256,256]{3,2,1,0:T(8,128)(2,1)}, u32[]{:S(2)}) copy-start(bf16[1,2,256,256]{3,2,1,0:T(8,128)(2,1)} %param.13) | copy-start | bytes 786436
  134.8 202.9 %all-gather.9.cloned.1.call-start = ((), (), s32[]{:S(2)}) async-start(), calls=%async_computation.2 | async-start | bytes 4325376 | tf_op jit(solution)/shard_map/all_gather | solution.py:62
  244.9 11.6 %copy-start.5 = (bf16[256,256]{1,0:T(8,128)(2,1)S(1)}, bf16[256,256]{1,0:T(8,128)(2,1)}, u32[]{:S(2)}) copy-start(bf16[256,256]{1,0:T(8,128)(2,1)} %param.10) | copy-start | bytes 393220
  244.9 13.4 %copy-start.1 = (bf16[1,2,2,256,256]{4,3,2,1,0:T(8,128)(2,1)S(1)}, bf16[1,2,2,256,256]{4,3,2,1,0:T(8,128)(2,1)}, u32[]{:S(2)}) copy-start(bf16[1,2,2,256,256]{4,3,2,1,0:T(8,128)(2,1)} %param.11) | copy-start | bytes 1572868
  244.9 13.4 %copy-start.6 = (bf16[1,256,256]{2,1,0:T(8,128)(2,1)S(1)}, bf16[1,256,256]{2,1,0:T(8,128)(2,1)}, u32[]{:S(2)}) copy-start(bf16[1,256,256]{2,1,0:T(8,128)(2,1)} %param.9) | copy-start | bytes 393220
  252.0 4.4 collective-permute-start
  257.3 264.3 %all-reduce.3.cloned.1.call-start = ((), (), s32[]{:S(2)}) async-start(), calls=%async_computation.4 | async-start | bytes 1048576 | tf_op jit(solution)/shard_map/psum | solution.py:56
  368.6 9.3 %copy-start.2 = (bf16[256,256]{1,0:T(8,128)(2,1)S(1)}, bf16[256,256]{1,0:T(8,128)(2,1)}, u32[]{:S(2)}) copy-start(bf16[256,256]{1,0:T(8,128)(2,1)} %fusion.15) | copy-start | bytes 393220
  368.6 9.3 %copy-start.3 = (bf16[256,256]{1,0:T(8,128)(2,1)S(1)}, bf16[256,256]{1,0:T(8,128)(2,1)}, u32[]{:S(2)}) copy-start(bf16[256,256]{1,0:T(8,128)(2,1)} %fusion.16) | copy-start | bytes 393220
  368.6 9.3 %copy-start.4 = (bf16[256,256]{1,0:T(8,128)(2,1)S(1)}, bf16[256,256]{1,0:T(8,128)(2,1)}, u32[]{:S(2)}) copy-start(bf16[256,256]{1,0:T(8,128)(2,1)} %add_convert_fusion) | copy-start | bytes 393220
  376.7 226.5 %all-gather.11.cloned.1.call-start = ((), (), s32[]{:S(2)}) async-start(), calls=%async_computation.3 | async-start | bytes 4325376 | tf_op jit(solution)/shard_map/all_gather | solution.py:62
Sparse Core Ops, SparseCore 0:
  11.2 84.5 all-gather.4
  134.9 78.9 all-gather.6
  257.5 80.1 all-gather.8
  376.8 144.8 all-reduce.2
  524.5 78.6 all-gather.10
where the time goes:
time: 649 us; the launch traced here: 648 us
  waiting for transfers between devices  464 us (71%)
  local copies, waits for them, and re-layouts  86.5 us (13%)
  matrix products  75.5 us (12%)
  between operations  14.2 us (2%)
    all_gather x4, waiting for transfers between devices, shards(): gathered = lax.all_gather(image, 'rows', axis=0, tiled=True)  319 us
    psum x1, waiting for transfers between devices, shards(): weight_acc[layer] = weight_acc[layer] + lax.psum(term, 'rows')  142 us
    dot_general x4, local copies, waits for them, and re-layouts, tile_product(): jnp.einsum('kab,kbf->kaf', values, blocks, preferred_element_type=jnp.flo...  51 us
    dot_general x4, matrix products, tile_product(): jnp.einsum('kab,kbf->kaf', values, blocks, preferred_element_type=jnp.flo...  40.3 us
    gather x4, local copies, waits for them, and re-layouts, tile_product(): blocks = gathered.reshape(-1, tile, width)[index]  32.4 us
    dot_general x4, matrix products, tile_product(): jnp.einsum('ik,kaf->iaf', select, products, precision=lax.Precision.HIGHEST)  28.2 us
  transfers between devices with their start and end apart: 6, of which 6 were waited for; matrix products, arithmetic and copies ran while one was open for 2% of the time, Pallas kernels for 0%

commit v1 on v0

--- a/solution.py
+++ b/solution.py
@@ -59,7 +59,16 @@
                 + beta * jnp.dot(masked, weight.T, preferred_element_type=jnp.float32)
             ).astype(jnp.bfloat16)
             toward = toward + ALPHA * image.astype(jnp.float32)
-            gathered = lax.all_gather(image, "rows", axis=0, tiled=True)
+            _draw_waves = lambda mine, device_axis: jnp.concatenate(
+                jax.lax.all_to_all(
+                    jnp.stack([mine for _ in range(jax.lax.axis_size(device_axis))], axis=0),
+                    device_axis,
+                    0,
+                    0,
+                ),
+                axis=0,
+            )
+            gathered = _draw_waves(image, "rows")
             spread = tile_product(
                 gathered, tile_vals[0, tick], tile_row[0, tick], columns, count, row_tiles
             )

time: 649 us -> 681 us (1.049)
  blocking collectives: 0 us -> 101 us
  waiting for transfers between devices: 464 us -> 367 us
  starting transfers between devices: 2.79 us -> 28.6 us
    all_gather x4 -> x0, waiting for transfers between devices: 319 us -> none  [shards(): gathered = lax.all_gather(image, 'rows', axis=0, tiled=True)]
    all_to_all x0 -> x3, waiting for transfers between devices: none -> 190 us  [shards(): jax.lax.all_to_all(jnp.stack([mine for _ in range(jax.lax.axis_size(devic...]
    all_to_all x0 -> x1, blocking collectives: none -> 101 us  [shards(): jax.lax.all_to_all(jnp.stack([mine for _ in range(jax.lax.axis_size(devic...]
    psum x1, waiting for transfers between devices: 142 us -> 174 us  [shards(): weight_acc[layer] = weight_acc[layer] + lax.psum(term, 'rows')]
    all_to_all x0 -> x3, starting transfers between devices: none -> 26.3 us  [shards(): jax.lax.all_to_all(jnp.stack([mine for _ in range(jax.lax.axis_size(devic...]
    another operation x0 -> x4, local copies, waits for them, and re-layouts: none -> 7.82 us  [shards(): jnp.stack([mine for _ in range(jax.lax.axis_size(device_axis))], axis=0)]
  transfers between devices with their start and end apart: 6 -> 5, of which waited for: 6 -> 4; matrix products, arithmetic and copies ran while one was open for 2% -> 1% of each run, Pallas kernels for 0% -> 0%
where the time goes in v1:
time: 681 us; the launch traced here: 680 us
  waiting for transfers between devices  367 us (54%)
  blocking collectives  101 us (15%)
  local copies, waits for them, and re-layouts  92.9 us (14%)
  matrix products  72.8 us (11%)
  starting transfers between devices  28.6 us (4%)
  between operations  14.5 us (2%)
    all_to_all x3, waiting for transfers between devices, shards(): jax.lax.all_to_all(jnp.stack([mine for _ in range(jax.lax.axis_size(devic...  190 us
    psum x1, waiting for transfers between devices, shards(): weight_acc[layer] = weight_acc[layer] + lax.psum(term, 'rows')  174 us
    all_to_all x1, blocking collectives, shards(): jax.lax.all_to_all(jnp.stack([mine for _ in range(jax.lax.axis_size(devic...  101 us
    dot_general x4, local copies, waits for them, and re-layouts, tile_product(): jnp.einsum('kab,kbf->kaf', values, blocks, preferred_element_type=jnp.flo...  51 us
    dot_general x4, matrix products, tile_product(): jnp.einsum('kab,kbf->kaf', values, blocks, preferred_element_type=jnp.flo...  40.4 us
    gather x4, local copies, waits for them, and re-layouts, tile_product(): blocks = gathered.reshape(-1, tile, width)[index]  32.5 us
    dot_general x4, matrix products, tile_product(): jnp.einsum('ik,kaf->iaf', select, products, precision=lax.Precision.HIGHEST)  28.1 us
    all_to_all x3, starting transfers between devices, shards(): jax.lax.all_to_all(jnp.stack([mine for _ in range(jax.lax.axis_size(devic...  26.3 us
  transfers between devices with their start and end apart: 5, of which 4 were waited for; matrix products, arithmetic and copies ran while one was open for 1% of the time, Pallas kernels for 0%

profile of v1, /device:TPU:8, one launch (start us, length us, event | category | flops | bytes accessed | tf_op | source)
XLA Modules:
  0.0 680.3 jit_solution(43178214722752357)
XLA Ops:
  11.1 11.4 %all-to-all-start = ((bf16[32,256,256]{2,1,0:T(8,128)(2,1)}), bf16[32,256,256]{2,1,0:T(8,128)(2,1)}, u32[]{:S(2)}, u32[]{:S(2)}) async-start(bf16[32,256,256]{2,1,0:T(8,128)(2,1)} %stack.22), calls=%async_computation | async-start | bytes 8388608 | tf_op jit(solution)/shard_map/all_to_all | solution.py:63
  24.0 95.8 %all-to-all-done = bf16[32,256,256]{2,1,0:T(8,128)(2,1)} async-done(((bf16[32,256,256]{2,1,0:T(8,128)(2,1)}), bf16[32,256,256]{2,1,0:T(8,128)(2,1)}, u32[]{:S(2)}, u32[]{:S(2)}) %all-to-all-start) | async-done | bytes 4194336 | tf_op jit(solution)/shard_map/all_to_all | solution.py:63
  119.8 8.1 %gather_fusion = bf16[96,128,256]{2,1,0:T(8,128)(2,1)} fusion(bf16[64,128,256]{2,1,0:T(8,128)(2,1)} %bitcast.9, s32[1024]{0:T(1024)S(1)} %pad_clamp_fusion.1), kind=kCustom, calls=%fused_computation | custom fusion | bytes 12583296 | tf_op jit(solution)/shard_map/gather | solution.py:19
  127.9 10.1 %convolution_bitcast_fusion.3 = f32[96,128,256]{1,2,0:T(8,128)} fusion(bf16[96,128,256]{2,1,0:T(8,128)(2,1)} %gather_fusion, bf16[1,2,96,128,128]{4,3,2,1,0:T(8,128)(2,1)} %param.14), kind=kOutput, calls=%fused_computation.7 | convolution fusion | flops 805306368 | bytes 22020096 | tf_op jit(solution)/shard_map/kab,kbf->kaf/dot_general | solution.py:20
  138.0 12.7 %copy.38 = f32[96,128,256]{2,0,1:T(8,128)} copy(f32[96,128,256]{1,2,0:T(8,128)} %convolution_bitcast_fusion.3) | data formatting | bytes 25165824 | tf_op jit(solution)/shard_map/kab,kbf->kaf/dot_general | solution.py:20
  150.8 7.1 %fusion.65 = f32[2,128,256]{2,0,1:T(2,128)S(1)} fusion(f32[96,128,256]{2,0,1:T(8,128)} %copy.38, pred[96]{0:T(512)(128)(4,1)S(1)} %iota_compare_fusion.1, s32[96]{0:T(128)S(1)} %get-tuple-element.18), kind=kOutput, calls=%fused_computation.97 | convolution fusion | flops 75497856 | bytes 12845536 | tf_op jit(solution)/shard_map/ik,kaf->iaf/dot_general | solution.py:25
  158.6 100.8 %all_to_all.20 = bf16[32,256,256]{2,1,0:T(8,128)(2,1)} all-to-all(bf16[32,256,256]{2,1,0:T(8,128)(2,1)S(1)} %stack.23), channel_id=1, replica_groups=mesh['section'=8,'rows'=32] {'rows'}, dimensions={0} | all-to-all | bytes 8388608 | tf_op jit(solution)/shard_map/all_to_all | solution.py:63
  259.4 8.1 %gather_fusion.1 = bf16[96,128,256]{2,1,0:T(8,128)(2,1)} fusion(bf16[64,128,256]{2,1,0:T(8,128)(2,1)} %bitcast.141, s32[1024]{0:T(1024)S(1)} %pad_clamp_fusion.1), kind=kCustom, calls=%fused_computation.1 | custom fusion | bytes 12583296 | tf_op jit(solution)/shard_map/gather | solution.py:19
  267.5 10.1 %convolution_bitcast_fusion.2 = f32[96,128,256]{1,2,0:T(8,128)} fusion(bf16[96,128,256]{2,1,0:T(8,128)(2,1)} %gather_fusion.1, bf16[1,2,96,128,128]{4,3,2,1,0:T(8,128)(2,1)} %param.14), kind=kOutput, calls=%fused_computation.6 | convolution fusion | flops 805306368 | bytes 22020096 | tf_op jit(solution)/shard_map/kab,kbf->kaf/dot_general | solution.py:20
  277.6 12.7 %copy.41 = f32[96,128,256]{2,0,1:T(8,128)} copy(f32[96,128,256]{1,2,0:T(8,128)} %convolution_bitcast_fusion.2) | data formatting | bytes 25165824 | tf_op jit(solution)/shard_map/kab,kbf->kaf/dot_general | solution.py:20
  290.4 7.0 %fusion.63 = f32[2,128,256]{2,0,1:T(2,128)S(1)} fusion(f32[96,128,256]{2,0,1:T(8,128)} %copy.41, pred[96]{0:T(512)(128)(4,1)S(1)} %iota_compare_fusion.1, s32[96]{0:T(128)S(1)} %get-tuple-element.18), kind=kOutput, calls=%fused_computation.95 | convolution fusion | flops 75497856 | bytes 12845536 | tf_op jit(solution)/shard_map/ik,kaf->iaf/dot_general | solution.py:25
  299.4 2.5 collective-permute-done
  304.6 5.3 all-to-all-start.2
  310.6 94.6 %all-to-all-done.2 = bf16[32,256,256]{2,1,0:T(8,128)(2,1)} async-done(((bf16[32,256,256]{2,1,0:T(8,128)(2,1)}), bf16[32,256,256]{2,1,0:T(8,128)(2,1)}, u32[]{:S(2)}, u32[]{:S(2)}) %all-to-all-start.2) | async-done | bytes 4194336 | tf_op jit(solution)/shard_map/all_to_all | solution.py:63
  405.2 8.1 %gather_fusion.2 = bf16[96,128,256]{2,1,0:T(8,128)(2,1)} fusion(bf16[64,128,256]{2,1,0:T(8,128)(2,1)} %bitcast.27, s32[1024]{0:T(1024)S(1)} %pad_clamp_fusion), kind=kCustom, calls=%fused_computation.2 | custom fusion | bytes 12583296 | tf_op jit(solution)/shard_map/gather | solution.py:19
  413.3 10.1 %convolution_bitcast_fusion.1 = f32[96,128,256]{1,2,0:T(8,128)} fusion(bf16[96,128,256]{2,1,0:T(8,128)(2,1)} %gather_fusion.2, bf16[1,2,96,128,128]{4,3,2,1,0:T(8,128)(2,1)} %param.14), kind=kOutput, calls=%fused_computation.5 | convolution fusion | flops 805306368 | bytes 22020096 | tf_op jit(solution)/shard_map/kab,kbf->kaf/dot_general | solution.py:20
  423.4 12.7 %copy.44 = f32[96,128,256]{2,0,1:T(8,128)} copy(f32[96,128,256]{1,2,0:T(8,128)} %convolution_bitcast_fusion.1) | data formatting | bytes 25165824 | tf_op jit(solution)/shard_map/kab,kbf->kaf/dot_general | solution.py:20
  436.2 7.0 %fusion.61 = f32[2,128,256]{2,0,1:T(2,128)S(1)} fusion(f32[96,128,256]{2,0,1:T(8,128)} %copy.44, pred[96]{0:T(512)(128)(4,1)S(1)} %iota_compare_fusion, s32[96]{0:T(128)S(1)} %get-tuple-element.17), kind=kOutput, calls=%fused_computation.93 | convolution fusion | flops 75497856 | bytes 12845536 | tf_op jit(solution)/shard_map/ik,kaf->iaf/dot_general | solution.py:25
  445.9 9.6 %all-to-all-start.3 = ((bf16[32,256,256]{2,1,0:T(8,128)(2,1)}), bf16[32,256,256]{2,1,0:T(8,128)(2,1)}, u32[]{:S(2)}, u32[]{:S(2)}) async-start(bf16[32,256,256]{2,1,0:T(8,128)(2,1)} %stack.25), calls=%async_computation.3 | async-start | bytes 8388608 | tf_op jit(solution)/shard_map/all_to_all | solution.py:63
  459.1 173.6 %all-reduce.3.cloned.1.call-done = (f32[256,256]{0,1:T(8,128)}, f32[256,256]{0,1:T(8,128)}) async-done(((f32[256,256]{0,1:T(8,128)}, f32[256,256]{0,1:T(8,128)}), (f32[256,256]{0,1:T(8,128)}, f32[256,256]{0,1:T(8,128)})) %all-reduce.3.cloned.1.call-update) | async-done | bytes 524304 | tf_op jit(solution)/shard_map/psum | solution.py:56
  634.8 8.1 %gather_fusion.3 = bf16[96,128,256]{2,1,0:T(8,128)(2,1)} fusion(bf16[64,128,256]{2,1,0:T(8,128)(2,1)} %bitcast.35, s32[1024]{0:T(1024)S(1)} %pad_clamp_fusion), kind=kCustom, calls=%fused_computation.3 | custom fusion | bytes 12583296 | tf_op jit(solution)/shard_map/gather | solution.py:19
  642.9 10.1 %convolution_bitcast_fusion = f32[96,128,256]{1,2,0:T(8,128)} fusion(bf16[96,128,256]{2,1,0:T(8,128)(2,1)} %gather_fusion.3, bf16[1,2,96,128,128]{4,3,2,1,0:T(8,128)(2,1)} %param.14), kind=kOutput, calls=%fused_computation.4 | convolution fusion | flops 805306368 | bytes 22020096 | tf_op jit(solution)/shard_map/kab,kbf->kaf/dot_general | solution.py:20
  653.0 12.7 %copy.47 = f32[96,128,256]{2,0,1:T(8,128)} copy(f32[96,128,256]{1,2,0:T(8,128)} %convolution_bitcast_fusion) | data formatting | bytes 25165824 | tf_op jit(solution)/shard_map/kab,kbf->kaf/dot_general | solution.py:20
  665.7 7.0 %fusion.59 = f32[2,128,256]{2,0,1:T(2,128)S(1)} fusion(f32[96,128,256]{2,0,1:T(8,128)} %copy.47, pred[96]{0:T(512)(128)(4,1)S(1)} %iota_compare_fusion, s32[96]{0:T(128)S(1)} %get-tuple-element.17), kind=kOutput, calls=%fused_computation.91 | convolution fusion | flops 75497856 | bytes 12845536 | tf_op jit(solution)/shard_map/ik,kaf->iaf/dot_general | solution.py:25
  (50 shorter events, 20.2 us)
Async XLA Ops:
  8.7 14.0 %copy-start.4 = (s32[1,2,1]{1,2,0:T(1,128)S(1)}, s32[1,2,1]{1,2,0:T(1,128)}, u32[]{:S(2)}) copy-start(s32[1,2,1]{1,2,0:T(1,128)} %param.17) | copy-start | bytes 28
  8.7 15.3 %copy-start.5 = (s32[1,2,96]{2,1,0:T(2,128)S(1)}, s32[1,2,96]{2,1,0:T(2,128)}, u32[]{:S(2)}) copy-start(s32[1,2,96]{2,1,0:T(2,128)} %param.16) | copy-start | bytes 2308
  8.7 15.3 %copy-start.6 = (s32[1,2,96]{2,1,0:T(2,128)S(1)}, s32[1,2,96]{2,1,0:T(2,128)}, u32[]{:S(2)}) copy-start(s32[1,2,96]{2,1,0:T(2,128)} %param.15) | copy-start | bytes 2308
  11.1 108.7 %all-to-all-start = ((bf16[32,256,256]{2,1,0:T(8,128)(2,1)}), bf16[32,256,256]{2,1,0:T(8,128)(2,1)}, u32[]{:S(2)}, u32[]{:S(2)}) async-start(bf16[32,256,256]{2,1,0:T(8,128)(2,1)} %stack.22), calls=%async_computation | async-start | bytes 8388608 | tf_op jit(solution)/shard_map/all_to_all | solution.py:63
  150.8 7.1 %copy-start = (bf16[1,2,2,256,256]{4,3,2,1,0:T(8,128)(2,1)S(1)}, bf16[1,2,2,256,256]{4,3,2,1,0:T(8,128)(2,1)}, u32[]{:S(2)}) copy-start(bf16[1,2,2,256,256]{4,3,2,1,0:T(8,128)(2,1)} %param.12) | copy-start | bytes 1572868
  150.8 7.1 %copy-start.7 = (bf16[1,2,256,256]{3,2,1,0:T(8,128)(2,1)S(1)}, bf16[1,2,256,256]{3,2,1,0:T(8,128)(2,1)}, u32[]{:S(2)}) copy-start(bf16[1,2,256,256]{3,2,1,0:T(8,128)(2,1)} %param.13) | copy-start | bytes 786436
  290.4 11.5 %copy-start.2 = (bf16[256,256]{1,0:T(8,128)(2,1)S(1)}, bf16[256,256]{1,0:T(8,128)(2,1)}, u32[]{:S(2)}) copy-start(bf16[256,256]{1,0:T(8,128)(2,1)} %param.10) | copy-start | bytes 393220
  297.5 4.4 collective-permute-start
  304.6 100.6 %all-to-all-start.2 = ((bf16[32,256,256]{2,1,0:T(8,128)(2,1)}), bf16[32,256,256]{2,1,0:T(8,128)(2,1)}, u32[]{:S(2)}, u32[]{:S(2)}) async-start(bf16[32,256,256]{2,1,0:T(8,128)(2,1)} %stack.24), calls=%async_computation.2 | async-start | bytes 8388608 | tf_op jit(solution)/shard_map/all_to_all | solution.py:63
  443.4 12.4 %copy-start.1 = (bf16[1,2,2,256,256]{4,3,2,1,0:T(8,128)(2,1)S(1)}, bf16[1,2,2,256,256]{4,3,2,1,0:T(8,128)(2,1)}, u32[]{:S(2)}) copy-start(bf16[1,2,2,256,256]{4,3,2,1,0:T(8,128)(2,1)} %param.11) | copy-start | bytes 1572868
  443.5 12.4 %copy-start.3 = (bf16[1,256,256]{2,1,0:T(8,128)(2,1)S(1)}, bf16[1,256,256]{2,1,0:T(8,128)(2,1)}, u32[]{:S(2)}) copy-start(bf16[1,256,256]{2,1,0:T(8,128)(2,1)} %param.9) | copy-start | bytes 393220
  445.9 188.8 %all-to-all-start.3 = ((bf16[32,256,256]{2,1,0:T(8,128)(2,1)}), bf16[32,256,256]{2,1,0:T(8,128)(2,1)}, u32[]{:S(2)}, u32[]{:S(2)}) async-start(bf16[32,256,256]{2,1,0:T(8,128)(2,1)} %stack.25), calls=%async_computation.3 | async-start | bytes 8388608 | tf_op jit(solution)/shard_map/all_to_all | solution.py:63
  455.5 177.2 %all-reduce.3.cloned.1.call-start = ((), (), s32[]{:S(2)}) async-start(), calls=%async_computation.4 | async-start | bytes 1048576 | tf_op jit(solution)/shard_map/psum | solution.py:56
Sparse Core Ops, SparseCore 0:
  460.4 172.2 all-reduce.2
